TPU v7x, 512 devices: a whole 4x4x16 slice. The times are simulated.
512 devices in a mesh: lvl: 16 (over z), col: 32 (over y, x, core).
Axes of the slice: x: 4, y: 4, z: 16, core: 2. Of those that a mesh axis runs over, the one named last changes fastest.
Arguments:
- rhs: float32 [16, 1536, 128], P('lvl', 'col'), may hold values from -6 to 6
- panel: bfloat16 [16, 4, 1536, 1536], P('lvl', None, 'col'), may hold values from -0.078125 to 0.078125
- inverse_t: bfloat16 [16, 1536, 1536], P('lvl', 'col'), as said below
- pattern: int32 [16, 4, 12, 12], P('lvl'), may hold values 0 or 1
Outputs:
- sample: float32 [16, 1536, 128], P('lvl', 'col')
- solution: float32 [16, 1536, 128], P('lvl', 'col')
Inputs may be any that keep to these rules, and one draw needn't show every extreme that they name: `pattern`: 1 marks a 128 x 128 tile of a panel slot that is structurally nonzero. Each inverse_t[s] is upper triangular with a positive diagonal.
All inputs are finite; a program needn't handle non-finite values.
Results may differ from a plain program's by a relative error of at most 0.035.
Values may be sent and summed in bfloat16 or wider, within the bound.
A program may use at most 64 MiB of HBM per device.

v0:
```python
import jax
import jax.numpy as jnp
from jax import lax
from jax.sharding import PartitionSpec as P


def as_sent(x):

    def short(part):
        return part.astype(jnp.bfloat16) if part.dtype == jnp.float32 else part

    return jax.tree.map(short, x)


def level_rank(device_pos, levels):
    running = jnp.zeros((), jnp.int32)
    for exponent in range(1, levels + 1):
        running = running + ((device_pos + 1) % 2**exponent == 0).astype(jnp.int32)
    return running


def expand_pattern(pattern_own, row_start, row_count, full_width):
    tile_count = pattern_own.shape[1]
    tile_size = full_width // tile_count
    row_ids = row_start + lax.iota(jnp.int32, row_count)
    row_pick = (row_ids[:, None] // tile_size == lax.iota(jnp.int32, tile_count)[None, :]).astype(
        jnp.bfloat16
    )
    col_pick = (
        lax.iota(jnp.int32, full_width)[None, :] // tile_size
        == lax.iota(jnp.int32, tile_count)[:, None]
    ).astype(jnp.bfloat16)
    row_mask = jnp.einsum(
        "rb,kbc->krc",
        row_pick,
        pattern_own.astype(jnp.bfloat16),
        preferred_element_type=jnp.float32,
    ).astype(jnp.bfloat16)
    return jnp.einsum("krc,cn->krn", row_mask, col_pick, preferred_element_type=jnp.float32).astype(
        jnp.bfloat16
    )


def pick_member(everyone, member_pos, member_total):
    safe_pos = jnp.clip(member_pos, 0, member_total - 1)
    picked = lax.dynamic_index_in_dim(everyone, safe_pos, 0, keepdims=False)
    inside = jnp.logical_and(member_pos >= 0, member_pos < member_total)
    return jnp.where(inside, picked, jnp.zeros_like(picked))


def on_device(rhs, panel, inverse_t, pattern):
    member_total = lax.axis_size("lvl")
    levels = member_total.bit_length() - 1
    device_pos = lax.axis_index("lvl")
    column_pos = lax.axis_index("col")
    row_count = rhs.shape[1]
    rhs_count = rhs.shape[2]
    full_width = inverse_t.shape[2]
    height = level_rank(device_pos, levels)
    right_side = rhs[0]
    inverse_own = inverse_t[0]
    factor = panel[0] * expand_pattern(pattern[0], column_pos * row_count, row_count, full_width)
    sample = jnp.zeros((row_count, rhs_count), jnp.float32)
    upward = jnp.zeros((levels + 1, row_count, rhs_count), jnp.float32)
    for section_num in range(levels + 1):
        if section_num == 0:
            gathered = upward
        else:
            reach_dist = 2 ** (section_num - 1)
            everyone = lax.all_gather(as_sent(upward[None]), "lvl", axis=0, tiled=True)
            from_left = pick_member(everyone, device_pos - reach_dist, member_total)
            from_right = pick_member(everyone, device_pos + reach_dist, member_total)
            gathered = from_left + from_right
        active = height == section_num
        residual = (right_side - gathered[0]).astype(jnp.bfloat16)
        partial_sum = jnp.einsum(
            "ri,rn->in", inverse_own, residual, preferred_element_type=jnp.float32
        )
        solved_all = lax.psum(partial_sum.astype(jnp.bfloat16), "col").astype(jnp.float32)
        own_rows = lax.dynamic_slice_in_dim(solved_all, column_pos * row_count, row_count, 0)
        solved_half = solved_all.astype(jnp.bfloat16)
        sample = jnp.where(active, own_rows, sample)
        remain = levels - section_num
        if remain > 0:
            pushed = jnp.einsum(
                "krn,nm->krm", factor[:remain], solved_half, preferred_element_type=jnp.float32
            )
            upward = jnp.where(active, pushed + gathered[1 : remain + 1], 0.0)
    answer = jnp.zeros((row_count, rhs_count), jnp.float32)
    ancestry = jnp.zeros((levels, row_count, rhs_count), jnp.bfloat16)
    downward = ancestry
    for section_num in range(levels, -1, -1):
        remain = levels - section_num
        active = height == section_num
        if remain > 0:
            reach_dist = 2**section_num
            everyone = lax.all_gather(downward[None], "lvl", axis=0, tiled=True)
            parent_up = device_pos // (2 * reach_dist) % 2 == 0
            parent_pos = jnp.where(parent_up, device_pos + reach_dist, device_pos - reach_dist)
            received = pick_member(everyone, parent_pos, member_total)
            ancestry = ancestry.at[:remain].set(jnp.where(active, received, ancestry[:remain]))
            partial_adj = jnp.einsum(
                "krn,krm->nm",
                factor[:remain],
                ancestry[:remain],
                preferred_element_type=jnp.float32,
            )
            adjoint = lax.psum_scatter(
                partial_adj.astype(jnp.bfloat16), "col", scatter_dimension=0, tiled=True
            ).astype(jnp.float32)
            back_full = sample - adjoint
        else:
            back_full = sample
        back_whole = lax.all_gather(back_full.astype(jnp.bfloat16), "col", axis=0, tiled=True)
        solved = jnp.dot(inverse_own, back_whole, preferred_element_type=jnp.float32)
        answer = jnp.where(active, solved, answer)
        solved_half = solved.astype(jnp.bfloat16)
        if section_num > 0:
            downward = jnp.concatenate(
                [solved_half[None], ancestry[: levels - section_num]], axis=0
            )
    return (sample[None], answer[None])


def solution(mesh):
    in_specs = (
        P("lvl", "col", None),
        P("lvl", None, "col", None),
        P("lvl", "col", None),
        P("lvl", None, None, None),
    )
    out_specs = (P("lvl", "col", None), P("lvl", "col", None))
    return jax.shard_map(
        on_device, mesh=mesh, in_specs=in_specs, out_specs=out_specs, check_vma=False
    )
```

profile of v0, /device:TPU:1, one launch (start us, length us, event | category | flops | bytes accessed | tf_op | source)
XLA Modules:
  0.0 1450.9 jit_solution(16410489634673471)
XLA Ops:
  8.1 1.8 convolution_convert_fusion.6
  10.7 139.2 %all-reduce.7.cloned.1.call-done = bf16[1536,128]{1,0:T(8,128)(2,1)} async-done(((bf16[1536,128]{1,0:T(8,128)(2,1)}), bf16[1536,128]{1,0:T(8,128)(2,1)}) %all-reduce.7.cloned.1.call-update) | async-done | bytes 393232 | tf_op jit(solution)/shard_map/psum | solution.py:79
  149.9 1.3 fusion.8
  151.2 28.1 %all-gather = bf16[64,48,128]{2,1,0:T(8,128)(2,1)S(1)} all-gather(bf16[4,48,128]{2,1,0:T(8,128)(2,1)S(1)} %fusion.8), channel_id=2, replica_groups=mesh['lvl'=16,'col'=32] {'lvl'}, dimensions={0}, use_global_device_ids=true | all-gather | bytes 835584 | tf_op jit(solution)/shard_map/all_gather | solution.py:70
  179.3 1.1 fusion.4
  180.5 136.0 %all-reduce.9.cloned.1.call-done = bf16[1536,128]{1,0:T(8,128)(2,1)} async-done(((bf16[1536,128]{1,0:T(8,128)(2,1)}), bf16[1536,128]{1,0:T(8,128)(2,1)}) %all-reduce.9.cloned.1.call-update) | async-done | bytes 393232 | tf_op jit(solution)/shard_map/psum | solution.py:79
  316.5 1.3 fusion.10
  317.8 27.0 %all-gather.1 = bf16[48,48,128]{2,1,0:T(8,128)(2,1)S(1)} all-gather(bf16[3,48,128]{2,1,0:T(8,128)(2,1)S(1)} %fusion.10), channel_id=3, replica_groups=mesh['lvl'=16,'col'=32] {'lvl'}, dimensions={0}, use_global_device_ids=true | all-gather | bytes 626688 | tf_op jit(solution)/shard_map/all_gather | solution.py:70
  344.8 1.1 fusion.5
  346.0 135.6 %all-reduce.11.cloned.1.call-done = bf16[1536,128]{1,0:T(8,128)(2,1)} async-done(((bf16[1536,128]{1,0:T(8,128)(2,1)}), bf16[1536,128]{1,0:T(8,128)(2,1)}) %all-reduce.11.cloned.1.call-update) | async-done | bytes 393232 | tf_op jit(solution)/shard_map/psum | solution.py:79
  481.6 1.2 fusion.12
  482.8 26.0 %all-gather.2 = bf16[32,48,128]{2,1,0:T(8,128)(2,1)S(1)} all-gather(bf16[2,48,128]{2,1,0:T(8,128)(2,1)S(1)} %fusion.12), channel_id=4, replica_groups=mesh['lvl'=16,'col'=32] {'lvl'}, dimensions={0}, use_global_device_ids=true | all-gather | bytes 417792 | tf_op jit(solution)/shard_map/all_gather | solution.py:70
  510.0 135.7 %all-reduce.13.cloned.1.call-done = bf16[1536,128]{1,0:T(8,128)(2,1)} async-done(((bf16[1536,128]{1,0:T(8,128)(2,1)}), bf16[1536,128]{1,0:T(8,128)(2,1)}) %all-reduce.13.cloned.1.call-update) | async-done | bytes 393232 | tf_op jit(solution)/shard_map/psum | solution.py:79
  645.7 1.2 fusion.16
  646.9 24.3 %all-gather.3 = bf16[16,48,128]{2,1,0:T(8,128)(2,1)S(1)} all-gather(bf16[1,48,128]{2,1,0:T(8,128)(2,1)S(1)} %fusion.16), channel_id=5, replica_groups=mesh['lvl'=16,'col'=32] {'lvl'}, dimensions={0}, use_global_device_ids=true | all-gather | bytes 208896 | tf_op jit(solution)/shard_map/all_gather | solution.py:70
  671.2 1.1 fusion.7
  672.4 136.2 %all-reduce.15.cloned.1.call-done = bf16[1536,128]{1,0:T(8,128)(2,1)} async-done(((bf16[1536,128]{1,0:T(8,128)(2,1)}), bf16[1536,128]{1,0:T(8,128)(2,1)}) %all-reduce.15.cloned.1.call-update) | async-done | bytes 393232 | tf_op jit(solution)/shard_map/psum | solution.py:79
  809.4 25.8 %all_gather.43 = bf16[1536,128]{1,0:T(8,128)(2,1)S(1)} all-gather(bf16[48,128]{1,0:T(8,128)(2,1)S(1)} %get-tuple-element.62), channel_id=1, replica_groups=mesh['lvl'=16,'col'=32] {'col'}, dimensions={0}, use_global_device_ids=true | all-gather | bytes 405504 | tf_op jit(solution)/shard_map/all_gather | solution.py:114
  835.5 24.6 %all-gather.4 = bf16[768,128]{1,0:T(8,128)(2,1)S(1)} all-gather(bf16[48,128]{1,0:T(8,128)(2,1)S(1)} %convert_bitcast_fusion.3), channel_id=6, replica_groups=mesh['lvl'=16,'col'=32] {'lvl'}, dimensions={0}, use_global_device_ids=true | all-gather | bytes 208896 | tf_op jit(solution)/shard_map/all_gather | solution.py:97
  861.4 96.8 %reduce-scatter.5.cloned.1.call-done = bf16[48,128]{1,0:T(8,128)(2,1)} async-done(((bf16[1536,128]{1,0:T(8,128)(2,1)}), bf16[48,128]{1,0:T(8,128)(2,1)}) %reduce-scatter.5.cloned.1.call-update) | async-done | bytes 12304 | tf_op jit(solution)/shard_map/reduce_scatter | solution.py:108
  958.8 26.6 %all_gather.45 = bf16[1536,128]{1,0:T(8,128)(2,1)S(1)} all-gather(bf16[48,128]{1,0:T(8,128)(2,1)S(1)} %subtract_convert_fusion.3), channel_id=1, replica_groups=mesh['lvl'=16,'col'=32] {'col'}, dimensions={0}, use_global_device_ids=true | all-gather | bytes 405504 | tf_op jit(solution)/shard_map/all_gather | solution.py:114
  985.6 25.8 %all-gather.5 = bf16[32,48,128]{2,1,0:T(8,128)(2,1)S(1)} all-gather(bf16[2,48,128]{2,1,0:T(8,128)(2,1)S(1)} %pad_maximum_fusion.2), channel_id=7, replica_groups=mesh['lvl'=16,'col'=32] {'lvl'}, dimensions={0}, use_global_device_ids=true | all-gather | bytes 417792 | tf_op jit(solution)/shard_map/all_gather | solution.py:97
  1012.5 97.4 %reduce-scatter.7.cloned.1.call-done = bf16[48,128]{1,0:T(8,128)(2,1)} async-done(((bf16[1536,128]{1,0:T(8,128)(2,1)}), bf16[48,128]{1,0:T(8,128)(2,1)}) %reduce-scatter.7.cloned.1.call-update) | async-done | bytes 12304 | tf_op jit(solution)/shard_map/reduce_scatter | solution.py:108
  1110.7 26.3 %all_gather.47 = bf16[1536,128]{1,0:T(8,128)(2,1)S(1)} all-gather(bf16[48,128]{1,0:T(8,128)(2,1)S(1)} %subtract_convert_fusion.2), channel_id=1, replica_groups=mesh['lvl'=16,'col'=32] {'col'}, dimensions={0}, use_global_device_ids=true | all-gather | bytes 405504 | tf_op jit(solution)/shard_map/all_gather | solution.py:114
  1137.2 26.6 %all-gather.6 = bf16[48,48,128]{2,1,0:T(8,128)(2,1)S(1)} all-gather(bf16[3,48,128]{2,1,0:T(8,128)(2,1)S(1)} %pad_maximum_fusion.1), channel_id=8, replica_groups=mesh['lvl'=16,'col'=32] {'lvl'}, dimensions={0}, use_global_device_ids=true | all-gather | bytes 626688 | tf_op jit(solution)/shard_map/all_gather | solution.py:97
  1163.9 1.2 fusion.3
  1165.1 97.6 %reduce-scatter.9.cloned.1.call-done = bf16[48,128]{1,0:T(8,128)(2,1)} async-done(((bf16[1536,128]{1,0:T(8,128)(2,1)}), bf16[48,128]{1,0:T(8,128)(2,1)}) %reduce-scatter.9.cloned.1.call-update) | async-done | bytes 12304 | tf_op jit(solution)/shard_map/reduce_scatter | solution.py:108
  1263.4 26.3 %all_gather.49 = bf16[1536,128]{1,0:T(8,128)(2,1)S(1)} all-gather(bf16[48,128]{1,0:T(8,128)(2,1)S(1)} %subtract_convert_fusion.1), channel_id=1, replica_groups=mesh['lvl'=16,'col'=32] {'col'}, dimensions={0}, use_global_device_ids=true | all-gather | bytes 405504 | tf_op jit(solution)/shard_map/all_gather | solution.py:114
  1289.9 27.8 %all-gather.7 = bf16[64,48,128]{2,1,0:T(8,128)(2,1)S(1)} all-gather(bf16[4,48,128]{2,1,0:T(8,128)(2,1)S(1)} %pad_maximum_fusion), channel_id=9, replica_groups=mesh['lvl'=16,'col'=32] {'lvl'}, dimensions={0}, use_global_device_ids=true | all-gather | bytes 835584 | tf_op jit(solution)/shard_map/all_gather | solution.py:97
  1317.7 1.2 fusion.1
  1318.9 97.7 %reduce-scatter.11.cloned.1.call-done = bf16[48,128]{1,0:T(8,128)(2,1)} async-done(((bf16[1536,128]{1,0:T(8,128)(2,1)}), bf16[48,128]{1,0:T(8,128)(2,1)}) %reduce-scatter.11.cloned.1.call-update) | async-done | bytes 12304 | tf_op jit(solution)/shard_map/reduce_scatter | solution.py:108
  1417.3 26.3 %all_gather.51 = bf16[1536,128]{1,0:T(8,128)(2,1)S(1)} all-gather(bf16[48,128]{1,0:T(8,128)(2,1)S(1)} %subtract_convert_fusion), channel_id=1, replica_groups=mesh['lvl'=16,'col'=32] {'col'}, dimensions={0}, use_global_device_ids=true | all-gather | bytes 405504 | tf_op jit(solution)/shard_map/all_gather | solution.py:114
  (59 shorter events, 10.5 us)
Async XLA Ops:
  7.2 0.9 copy-start
  7.2 2.9 copy-start.4
  7.2 2.9 copy-start.3
  7.2 142.7 %all-reduce.7.cloned.1.call-start = ((), (), s32[]{:S(2)}) async-start(), calls=%async_computation.4 | async-start | bytes 786432 | tf_op jit(solution)/shard_map/psum | solution.py:79
  9.9 306.6 %all-reduce.9.cloned.1.call-start = ((), (), s32[]{:S(2)}) async-start(), calls=%async_computation.5 | async-start | bytes 786432 | tf_op jit(solution)/shard_map/psum | solution.py:79
  10.7 168.6 %copy-start.1 = (f32[1,48,128]{2,1,0:T(8,128)S(1)}, f32[1,48,128]{2,1,0:T(8,128)}, u32[]{:S(2)}) copy-start(f32[1,48,128]{2,1,0:T(8,128)} %param.14) | copy-start | bytes 73732
  180.5 301.1 %all-reduce.11.cloned.1.call-start = ((), (), s32[]{:S(2)}) async-start(), calls=%async_computation.6 | async-start | bytes 786432 | tf_op jit(solution)/shard_map/psum | solution.py:79
  345.9 299.8 %all-reduce.13.cloned.1.call-start = ((), (), s32[]{:S(2)}) async-start(), calls=%async_computation.7 | async-start | bytes 786432 | tf_op jit(solution)/shard_map/psum | solution.py:79
  509.9 298.7 %all-reduce.15.cloned.1.call-start = ((), (), s32[]{:S(2)}) async-start(), calls=%async_computation.8 | async-start | bytes 786432 | tf_op jit(solution)/shard_map/psum | solution.py:79
  672.3 285.8 %reduce-scatter.5.cloned.1.call-start = ((), (), s32[]{:S(2)}) async-start(), calls=%async_computation.9 | async-start | bytes 405504 | tf_op jit(solution)/shard_map/reduce_scatter | solution.py:108
  809.4 607.1 %copy-start.2 = (f32[48,128]{1,0:T(8,128)}, f32[48,128]{1,0:T(8,128)S(1)}, u32[]{:S(2)}) copy-start(f32[48,128]{1,0:T(8,128)S(1)} %get-tuple-element.63) | copy-start | bytes 73732
  861.2 248.8 %reduce-scatter.7.cloned.1.call-start = ((), (), s32[]{:S(2)}) async-start(), calls=%async_computation.10 | async-start | bytes 405504 | tf_op jit(solution)/shard_map/reduce_scatter | solution.py:108
  1012.5 250.2 %reduce-scatter.9.cloned.1.call-start = ((), (), s32[]{:S(2)}) async-start(), calls=%async_computation.11 | async-start | bytes 405504 | tf_op jit(solution)/shard_map/reduce_scatter | solution.py:108
  1165.0 251.5 %reduce-scatter.11.cloned.1.call-start = ((), (), s32[]{:S(2)}) async-start(), calls=%async_computation.12 | async-start | bytes 405504 | tf_op jit(solution)/shard_map/reduce_scatter | solution.py:108
Sparse Core Ops, SparseCore 0:
  11.2 138.5 all-reduce.6
  180.6 135.8 all-reduce.8
  346.0 135.5 all-reduce.10
  510.0 135.6 all-reduce.12
  672.4 136.1 all-reduce.14
  861.3 96.7 reduce-scatter.4
  1012.6 97.3 reduce-scatter.6
  1165.2 97.4 reduce-scatter.8
  1319.0 97.5 reduce-scatter.10
where the time goes:
time: 1450 us
  waiting for transfers between devices  1070 us (74%)
  blocking collectives  341 us (24%)
  matrix products  17.7 us (1%)
    psum x5, waiting for transfers between devices, on_device(): lax.psum(partial_sum.astype(jnp.bfloat16), 'col').astype(jnp.float32)  683 us
    reduce_scatter x4, waiting for transfers between devices, on_device(): lax.psum_scatter(partial_adj.astype(jnp.bfloat16), 'col', scatter_dimensi...  389 us
    all_gather x5, blocking collectives, on_device(): lax.all_gather(back_full.astype(jnp.bfloat16), 'col', axis=0, tiled=True)  131 us
    all_gather x4, blocking collectives, on_device(): everyone = lax.all_gather(as_sent(upward[None]), 'lvl', axis=0, tiled=True)  105 us
    all_gather x4, blocking collectives, on_device(): everyone = lax.all_gather(downward[None], 'lvl', axis=0, tiled=True)  105 us
  transfers between devices with their start and end apart: 9, of which 9 were waited for; matrix products, arithmetic and copies ran while one was open for 0% of the time, Pallas kernels for 0%

commit v1 on v0

--- a/solution.py
+++ b/solution.py
@@ -94,7 +94,18 @@
         active = height == section_num
         if remain > 0:
             reach_dist = 2**section_num
-            everyone = lax.all_gather(downward[None], "lvl", axis=0, tiled=True)
+            ways = lax.axis_size("lvl")
+            up = [(d, (d + 1) % ways) for d in range(ways)]
+            down = [(d, (d - 1) % ways) for d in range(ways)]
+            earlier, later = ([downward[None]], [downward[None]])
+            for _ in range(ways // 2):
+                earlier.append(lax.ppermute(earlier[-1], "lvl", up))
+            for _ in range((ways - 1) // 2):
+                later.append(lax.ppermute(later[-1], "lvl", down))
+            line = jnp.concatenate([*earlier[::-1], *later[1:]], axis=0)
+            everyone = jnp.roll(
+                line, (lax.axis_index("lvl") - ways // 2) * downward[None].shape[0], axis=0
+            )
             parent_up = device_pos // (2 * reach_dist) % 2 == 0
             parent_pos = jnp.where(parent_up, device_pos + reach_dist, device_pos - reach_dist)
             received = pick_member(everyone, parent_pos, member_total)

time: 1450 us -> 1570 us (1.083)
  starting transfers between devices: 0.37 us -> 195 us
  blocking collectives: 341 us -> 237 us
  waiting for transfers between devices: 1070 us -> 1100 us
    ppermute x0 -> x60, starting transfers between devices: none -> 195 us  [the longest x28 128 us: on_device(): later.append(lax.ppermute(later[-1], 'lvl', down))]
    all_gather x4 -> x0, blocking collectives: 105 us -> none  [on_device(): everyone = lax.all_gather(downward[None], 'lvl', axis=0, tiled=True)]
    ppermute x0 -> x60, waiting for transfers between devices: none -> 19 us  [the longest x32 15.9 us: on_device(): earlier.append(lax.ppermute(earlier[-1], 'lvl', up))]
  transfers between devices with their start and end apart: 9 -> 69, of which waited for: 9 -> 17; matrix products, arithmetic and copies ran while one was open for 0% -> 0% of each run, Pallas kernels for 0% -> 0%
where the time goes in v1:
time: 1570 us
  waiting for transfers between devices  1100 us (70%)
  blocking collectives  237 us (15%)
  starting transfers between devices  195 us (12%)
  matrix products  17.7 us (1%)
  between operations  15.9 us (1%)
    psum x5, waiting for transfers between devices, on_device(): lax.psum(partial_sum.astype(jnp.bfloat16), 'col').astype(jnp.float32)  682 us
    reduce_scatter x4, waiting for transfers between devices, on_device(): lax.psum_scatter(partial_adj.astype(jnp.bfloat16), 'col', scatter_dimensi...  399 us
    all_gather x5, blocking collectives, on_device(): lax.all_gather(back_full.astype(jnp.bfloat16), 'col', axis=0, tiled=True)  131 us
    ppermute x28, starting transfers between devices, on_device(): later.append(lax.ppermute(later[-1], 'lvl', down))  128 us
    all_gather x4, blocking collectives, on_device(): everyone = lax.all_gather(as_sent(upward[None]), 'lvl', axis=0, tiled=True)  105 us
    ppermute x32, starting transfers between devices, on_device(): earlier.append(lax.ppermute(earlier[-1], 'lvl', up))  66.5 us
  transfers between devices with their start and end apart: 69, of which 17 were waited for; matrix products, arithmetic and copies ran while one was open for 0% of the time, Pallas kernels for 0%

profile of v1, /device:TPU:1, one launch (start us, length us, event | category | flops | bytes accessed | tf_op | source)
XLA Modules:
  0.0 1572.0 jit_solution(17528025708450450407)
XLA Ops:
  11.4 138.5 %all-reduce.7.cloned.1.call-done = bf16[1536,128]{1,0:T(8,128)(2,1)} async-done(((bf16[1536,128]{1,0:T(8,128)(2,1)}), bf16[1536,128]{1,0:T(8,128)(2,1)}) %all-reduce.7.cloned.1.call-update) | async-done | bytes 393232 | tf_op jit(solution)/shard_map/psum | solution.py:79
  151.2 28.1 %all-gather = bf16[64,48,128]{2,1,0:T(8,128)(2,1)S(1)} all-gather(bf16[4,48,128]{2,1,0:T(8,128)(2,1)S(1)} %fusion.8), channel_id=2, replica_groups=mesh['lvl'=16,'col'=32] {'lvl'}, dimensions={0}, use_global_device_ids=true | all-gather | bytes 835584 | tf_op jit(solution)/shard_map/all_gather | solution.py:70
  180.5 136.0 %all-reduce.9.cloned.1.call-done = bf16[1536,128]{1,0:T(8,128)(2,1)} async-done(((bf16[1536,128]{1,0:T(8,128)(2,1)}), bf16[1536,128]{1,0:T(8,128)(2,1)}) %all-reduce.9.cloned.1.call-update) | async-done | bytes 393232 | tf_op jit(solution)/shard_map/psum | solution.py:79
  317.7 27.0 %all-gather.1 = bf16[48,48,128]{2,1,0:T(8,128)(2,1)S(1)} all-gather(bf16[3,48,128]{2,1,0:T(8,128)(2,1)S(1)} %fusion.10), channel_id=3, replica_groups=mesh['lvl'=16,'col'=32] {'lvl'}, dimensions={0}, use_global_device_ids=true | all-gather | bytes 626688 | tf_op jit(solution)/shard_map/all_gather | solution.py:70
  345.9 135.6 %all-reduce.11.cloned.1.call-done = bf16[1536,128]{1,0:T(8,128)(2,1)} async-done(((bf16[1536,128]{1,0:T(8,128)(2,1)}), bf16[1536,128]{1,0:T(8,128)(2,1)}) %all-reduce.11.cloned.1.call-update) | async-done | bytes 393232 | tf_op jit(solution)/shard_map/psum | solution.py:79
  482.8 26.0 %all-gather.2 = bf16[32,48,128]{2,1,0:T(8,128)(2,1)S(1)} all-gather(bf16[2,48,128]{2,1,0:T(8,128)(2,1)S(1)} %fusion.12), channel_id=4, replica_groups=mesh['lvl'=16,'col'=32] {'lvl'}, dimensions={0}, use_global_device_ids=true | all-gather | bytes 417792 | tf_op jit(solution)/shard_map/all_gather | solution.py:70
  510.0 135.7 %all-reduce.13.cloned.1.call-done = bf16[1536,128]{1,0:T(8,128)(2,1)} async-done(((bf16[1536,128]{1,0:T(8,128)(2,1)}), bf16[1536,128]{1,0:T(8,128)(2,1)}) %all-reduce.13.cloned.1.call-update) | async-done | bytes 393232 | tf_op jit(solution)/shard_map/psum | solution.py:79
  646.8 24.3 %all-gather.3 = bf16[16,48,128]{2,1,0:T(8,128)(2,1)S(1)} all-gather(bf16[1,48,128]{2,1,0:T(8,128)(2,1)S(1)} %fusion.16), channel_id=5, replica_groups=mesh['lvl'=16,'col'=32] {'lvl'}, dimensions={0}, use_global_device_ids=true | all-gather | bytes 208896 | tf_op jit(solution)/shard_map/all_gather | solution.py:70
  672.3 136.2 %all-reduce.15.cloned.1.call-done = bf16[1536,128]{1,0:T(8,128)(2,1)} async-done(((bf16[1536,128]{1,0:T(8,128)(2,1)}), bf16[1536,128]{1,0:T(8,128)(2,1)}) %all-reduce.15.cloned.1.call-update) | async-done | bytes 393232 | tf_op jit(solution)/shard_map/psum | solution.py:79
  809.3 25.8 %all_gather.31 = bf16[1536,128]{1,0:T(8,128)(2,1)S(1)} all-gather(bf16[48,128]{1,0:T(8,128)(2,1)S(1)} %get-tuple-element.62), channel_id=1, replica_groups=mesh['lvl'=16,'col'=32] {'col'}, dimensions={0}, use_global_device_ids=true | all-gather | bytes 405504 | tf_op jit(solution)/shard_map/all_gather | solution.py:125
  844.0 4.6 collective-permute-start.8
  850.6 4.6 collective-permute-start.9
  857.1 4.6 collective-permute-start.10
  863.6 4.6 collective-permute-start.11
  870.1 4.6 collective-permute-start.12
  876.7 4.6 collective-permute-start.13
  890.0 99.6 %reduce-scatter.5.cloned.1.call-done = bf16[48,128]{1,0:T(8,128)(2,1)} async-done(((bf16[1536,128]{1,0:T(8,128)(2,1)}), bf16[48,128]{1,0:T(8,128)(2,1)}) %reduce-scatter.5.cloned.1.call-update) | async-done | bytes 12304 | tf_op jit(solution)/shard_map/reduce_scatter | solution.py:119
  990.4 26.3 %all_gather.32 = bf16[1536,128]{1,0:T(8,128)(2,1)S(1)} all-gather(bf16[48,128]{1,0:T(8,128)(2,1)S(1)} %subtract_convert_fusion.3), channel_id=1, replica_groups=mesh['lvl'=16,'col'=32] {'col'}, dimensions={0}, use_global_device_ids=true | all-gather | bytes 405504 | tf_op jit(solution)/shard_map/all_gather | solution.py:125
  1064.9 4.6 collective-permute-start.29
  1071.8 99.9 %reduce-scatter.7.cloned.1.call-done = bf16[48,128]{1,0:T(8,128)(2,1)} async-done(((bf16[1536,128]{1,0:T(8,128)(2,1)}), bf16[48,128]{1,0:T(8,128)(2,1)}) %reduce-scatter.7.cloned.1.call-update) | async-done | bytes 12304 | tf_op jit(solution)/shard_map/reduce_scatter | solution.py:119
  1172.3 26.3 %all_gather.33 = bf16[1536,128]{1,0:T(8,128)(2,1)S(1)} all-gather(bf16[48,128]{1,0:T(8,128)(2,1)S(1)} %subtract_convert_fusion.2), channel_id=1, replica_groups=mesh['lvl'=16,'col'=32] {'col'}, dimensions={0}, use_global_device_ids=true | all-gather | bytes 405504 | tf_op jit(solution)/shard_map/all_gather | solution.py:125
  1214.7 4.8 collective-permute-start.39
  1221.4 4.6 collective-permute-start.40
  1227.9 4.6 collective-permute-start.41
  1234.4 4.6 collective-permute-start.42
  1241.0 4.6 collective-permute-start.43
  1247.5 4.6 collective-permute-start.44
  1254.7 99.5 %reduce-scatter.9.cloned.1.call-done = bf16[48,128]{1,0:T(8,128)(2,1)} async-done(((bf16[1536,128]{1,0:T(8,128)(2,1)}), bf16[48,128]{1,0:T(8,128)(2,1)}) %reduce-scatter.9.cloned.1.call-update) | async-done | bytes 12304 | tf_op jit(solution)/shard_map/reduce_scatter | solution.py:119
  1354.9 26.3 %all_gather.34 = bf16[1536,128]{1,0:T(8,128)(2,1)S(1)} all-gather(bf16[48,128]{1,0:T(8,128)(2,1)S(1)} %subtract_convert_fusion.1), channel_id=1, replica_groups=mesh['lvl'=16,'col'=32] {'col'}, dimensions={0}, use_global_device_ids=true | all-gather | bytes 405504 | tf_op jit(solution)/shard_map/all_gather | solution.py:125
  1430.2 4.6 collective-permute-start.59
  1437.4 99.9 %reduce-scatter.11.cloned.1.call-done = bf16[48,128]{1,0:T(8,128)(2,1)} async-done(((bf16[1536,128]{1,0:T(8,128)(2,1)}), bf16[48,128]{1,0:T(8,128)(2,1)}) %reduce-scatter.11.cloned.1.call-update) | async-done | bytes 12304 | tf_op jit(solution)/shard_map/reduce_scatter | solution.py:119
  1538.1 26.6 %all_gather.35 = bf16[1536,128]{1,0:T(8,128)(2,1)S(1)} all-gather(bf16[48,128]{1,0:T(8,128)(2,1)S(1)} %subtract_convert_fusion), channel_id=1, replica_groups=mesh['lvl'=16,'col'=32] {'col'}, dimensions={0}, use_global_device_ids=true | all-gather | bytes 405504 | tf_op jit(solution)/shard_map/all_gather | solution.py:125
  (301 shorter events, 174.4 us)
Async XLA Ops:
  7.2 142.7 %all-reduce.7.cloned.1.call-start = ((), (), s32[]{:S(2)}) async-start(), calls=%async_computation.4 | async-start | bytes 786432 | tf_op jit(solution)/shard_map/psum | solution.py:79
  9.9 306.6 %all-reduce.9.cloned.1.call-start = ((), (), s32[]{:S(2)}) async-start(), calls=%async_computation.5 | async-start | bytes 786432 | tf_op jit(solution)/shard_map/psum | solution.py:79
  180.4 301.1 %all-reduce.11.cloned.1.call-start = ((), (), s32[]{:S(2)}) async-start(), calls=%async_computation.6 | async-start | bytes 786432 | tf_op jit(solution)/shard_map/psum | solution.py:79
  345.8 299.8 %all-reduce.13.cloned.1.call-start = ((), (), s32[]{:S(2)}) async-start(), calls=%async_computation.7 | async-start | bytes 786432 | tf_op jit(solution)/shard_map/psum | solution.py:79
  509.9 298.6 %all-reduce.15.cloned.1.call-start = ((), (), s32[]{:S(2)}) async-start(), calls=%async_computation.8 | async-start | bytes 786432 | tf_op jit(solution)/shard_map/psum | solution.py:79
  672.2 317.4 %reduce-scatter.5.cloned.1.call-start = ((), (), s32[]{:S(2)}) async-start(), calls=%async_computation.9 | async-start | bytes 405504 | tf_op jit(solution)/shard_map/reduce_scatter | solution.py:119
  835.4 6.7 collective-permute-start
  844.0 6.5 collective-permute-start.8
  848.6 6.5 collective-permute-start.2
  850.6 6.5 collective-permute-start.9
  855.1 6.5 collective-permute-start.3
  857.1 6.5 collective-permute-start.10
  861.7 6.5 collective-permute-start.4
  863.6 6.5 collective-permute-start.11
  868.2 6.5 collective-permute-start.5
  870.1 6.5 collective-permute-start.12
  876.7 6.6 collective-permute-start.13
  881.3 6.6 collective-permute-start.7
  890.0 281.7 %reduce-scatter.7.cloned.1.call-start = ((), (), s32[]{:S(2)}) async-start(), calls=%async_computation.10 | async-start | bytes 405504 | tf_op jit(solution)/shard_map/reduce_scatter | solution.py:119
  1016.8 6.9 collective-permute-start.15
  1058.3 6.6 collective-permute-start.28
  1062.9 6.6 collective-permute-start.22
  1071.7 282.5 %reduce-scatter.9.cloned.1.call-start = ((), (), s32[]{:S(2)}) async-start(), calls=%async_computation.11 | async-start | bytes 405504 | tf_op jit(solution)/shard_map/reduce_scatter | solution.py:119
  1198.9 7.4 collective-permute-start.30
  1212.7 6.7 collective-permute-start.32
  1214.7 6.7 collective-permute-start.39
  1241.0 6.6 collective-permute-start.43
  1245.6 6.6 collective-permute-start.37
  1254.7 282.7 %reduce-scatter.11.cloned.1.call-start = ((), (), s32[]{:S(2)}) async-start(), calls=%async_computation.12 | async-start | bytes 405504 | tf_op jit(solution)/shard_map/reduce_scatter | solution.py:119
  1381.4 7.6 collective-permute-start.45
  1423.6 6.6 collective-permute-start.58
  1428.2 6.6 collective-permute-start.52
  (41 other events, 1138.0 us)
Sparse Core Ops, SparseCore 0:
  11.2 138.5 all-reduce.6
  180.6 135.8 all-reduce.8
  346.0 135.5 all-reduce.10
  510.0 135.5 all-reduce.12
  672.4 136.0 all-reduce.14
  890.1 99.5 reduce-scatter.4
  1071.8 99.7 reduce-scatter.6
  1254.8 99.3 reduce-scatter.8
  1437.6 99.7 reduce-scatter.10
